TPU v7x, 32 devices: a whole 2x2x4 slice. The times are simulated.
32 devices in a mesh: sub: 4 (over z), blk: 8 (over y, x, core).
Axes of the slice: x: 2, y: 2, z: 4, core: 2. Of those that a mesh axis runs over, the one named last changes fastest.
Arguments:
- double_layer: bfloat16 [4, 2, 2048, 2048], P('sub', None, 'blk'), may hold values from -1 to 2
- single_layer: bfloat16 [4, 2, 2048, 2048], P('sub', None, 'blk'), may hold values from -1 to 2
- hypersingular: bfloat16 [4, 2, 2048, 2048], P('sub', None, 'blk'), may hold values from -1 to 2
- adjoint_double: bfloat16 [4, 2, 2048, 2048], P('sub', None, 'blk'), may hold values from -1 to 2
- matching: int32 [4, 1024], replicated, may hold values from 0 to 1023, each once within a row
- right_side: float32 [4, 2, 2, 2048, 64], P('sub', None, None, 'blk'), may hold values from -6 to 6
- start: float32 [4, 2, 2, 2048, 64], P('sub', None, None, 'blk'), may hold values from -4 to 4
Outputs:
- solution: float32 [4, 2, 2, 2048, 64], P('sub', None, None, 'blk')
Inputs may be any that keep to these rules, and one draw needn't show every extreme that they name: `matching`: each row is a permutation of 0 to 1023; row 0 pairs with no subdomain below and is not read.
All inputs are finite; a program needn't handle non-finite values.
Results may differ from a plain program's by a relative error of at most 0.015.
Values may be sent and summed in bfloat16 or wider, within the bound.
A program may use at most 64 MiB of HBM per device.

v0:
```python
import jax
import jax.numpy as jnp
from jax import lax
from jax.sharding import PartitionSpec as P

BASIS = 5


EPSILON = 1e-06


def passed_along(block, axis, distance):
    devices = range(lax.axis_size(axis))
    route = [(i - distance, i) for i in devices if i - distance in devices]
    return lax.ppermute(block, axis, route)


def complex_product(matrix, vector):
    width = vector.shape[-1] // 2
    count = matrix.shape[1]
    products = jnp.dot(
        matrix.reshape(2 * count, matrix.shape[2]), vector, preferred_element_type=jnp.float32
    )
    products = products.reshape(2, count, 2 * width)
    real_part = products[0, :, :width] - products[1, :, width:]
    imag_part = products[0, :, width:] + products[1, :, :width]
    return jnp.concatenate([real_part, imag_part], axis=-1)


def calderon(double_layer, single_layer, hypersingular, adjoint_double, vector):
    upper = complex_product(single_layer, vector[1]) - complex_product(double_layer, vector[0])
    lower = complex_product(hypersingular, vector[0]) + complex_product(adjoint_double, vector[1])
    return jnp.stack([upper, lower])


def inward(field):
    local_field = field[0]
    return jnp.concatenate([local_field[:, 0], local_field[:, 1]], axis=-1)


def outward(vector):
    width = vector.shape[-1] // 2
    return jnp.stack([vector[..., :width], vector[..., width:]], axis=1)[None]


def coupling_rows(gathered, matching, local_rows):
    subdomains = lax.axis_size("sub")
    own_index = lax.axis_index("sub")
    block_index = lax.axis_index("blk")
    half_rows = local_rows // 2
    above_index = jnp.minimum(own_index + 1, subdomains - 1)
    perm_here = lax.dynamic_index_in_dim(matching, own_index, 0, keepdims=False)
    perm_above = lax.dynamic_index_in_dim(matching, above_index, 0, keepdims=False)
    window = block_index * half_rows
    odd_rows = gathered[:, 1::2]
    even_rows = gathered[:, 0::2]
    odd_below = passed_along(odd_rows, "sub", 1)
    even_above = passed_along(even_rows, "sub", -1)
    inverse_above = jnp.argsort(perm_above)
    lower_face = jnp.take(odd_below, lax.dynamic_slice_in_dim(perm_here, window, half_rows), axis=1)
    upper_face = jnp.take(
        even_above, lax.dynamic_slice_in_dim(inverse_above, window, half_rows), axis=1
    )
    joined = jnp.stack([lower_face, upper_face], axis=2)
    joined = joined.reshape(2, local_rows, gathered.shape[-1]).astype(jnp.float32)
    trace_signs = jnp.array([1.0, -1.0], jnp.float32).reshape(2, 1, 1)
    return joined * trace_signs


def preconditioned(operators, matching, vector):
    rounded = vector.astype(jnp.bfloat16)
    gathered = lax.all_gather(rounded, "blk", axis=1, tiled=True)
    first_image = calderon(*operators, gathered)
    middle = first_image - 0.5 * coupling_rows(gathered, matching, vector.shape[1])
    middle_rounded = middle.astype(jnp.bfloat16)
    middle_full = lax.all_gather(middle_rounded, "blk", axis=1, tiled=True)
    return calderon(*operators, middle_full)


def inner_local(first, second):
    totals = jnp.sum(first * second, axis=(0, 1))
    width = totals.shape[0] // 2
    return totals[:width] + totals[width:]


def spread(values):
    return jnp.concatenate([values, values])


def global_norm(vector):
    return jnp.sqrt(lax.psum(inner_local(vector, vector), ("sub", "blk")) + EPSILON)


def body(double_layer, single_layer, hypersingular, adjoint_double, matching, right_side, start):
    operators = (double_layer[0], single_layer[0], hypersingular[0], adjoint_double[0])
    right_local = inward(right_side)
    start_local = inward(start)
    residual = right_local - preconditioned(operators, matching, start_local)
    beta = global_norm(residual)
    basis = [residual / spread(beta)]
    columns = []
    for column in range(BASIS):
        image = preconditioned(operators, matching, basis[column])
        local_dots = [inner_local(basis[earlier], image) for earlier in range(column + 1)]
        stacked_dots = jnp.stack(local_dots + [inner_local(image, image)])
        summed = lax.psum(stacked_dots, ("sub", "blk"))
        coefficients = [summed[earlier] for earlier in range(column + 1)]
        for earlier in range(column + 1):
            image = image - spread(coefficients[earlier]) * basis[earlier]
        squares = summed[column + 1] - jnp.sum(summed[: column + 1] * summed[: column + 1], axis=0)
        height = jnp.sqrt(jnp.maximum(squares, 0.0) + EPSILON)
        if column + 1 < BASIS:
            basis.append(image / spread(height))
        filler = [jnp.zeros_like(height)] * (BASIS - 1 - column)
        columns.append(jnp.stack(coefficients + [height] + filler, axis=1))
    hessen = jnp.stack(columns, axis=2)
    gram = jnp.einsum("rij,rik->rjk", hessen, hessen, precision=lax.Precision.HIGHEST)
    target = beta[:, None] * hessen[:, 0, :]
    factor = jnp.linalg.cholesky(gram)
    weights = jax.scipy.linalg.cho_solve((factor, True), target[..., None])[..., 0]
    solution = start_local
    for column in range(BASIS):
        solution = solution + spread(weights[:, column]) * basis[column]
    return outward(solution)


def solution(mesh):
    placed = (
        P("sub", None, "blk", None),
        P("sub", None, "blk", None),
        P("sub", None, "blk", None),
        P("sub", None, "blk", None),
        P(),
        P("sub", None, None, "blk", None),
        P("sub", None, None, "blk", None),
    )
    return jax.shard_map(
        body,
        mesh=mesh,
        in_specs=placed,
        out_specs=P("sub", None, None, "blk", None),
        check_vma=False,
    )
```

profile of v0, /device:TPU:0, one launch (start us, length us, event | category | flops | bytes accessed | tf_op | source)
XLA Modules:
  0.0 903.4 jit_solution(5222754914064992789)
XLA Ops:
  9.6 4.4 sort.27
  14.9 20.5 %all-gather.13.cloned.1.call-done = bf16[2,2048,128]{2,0,1:T(2,128)(2,1)} async-done(((bf16[2,256,128]{2,0,1:T(2,128)(2,1)}), bf16[2,2048,128]{2,0,1:T(2,128)(2,1)}) %all-gather.13.cloned.1.call-update) | async-done | bytes 1048592 | tf_op jit(solution)/shard_map/all_gather | solution.py:72
  35.4 4.1 fusion.59
  43.6 2.8 convolution_bitcast_fusion.45
  46.5 2.8 convolution_bitcast_fusion.44
  49.4 2.7 fusion.58
  53.4 5.4 collective-permute-start
  59.5 8.7 collective-permute-done.1
  74.2 23.6 %all-gather.15.cloned.1.call-done = bf16[2,2048,128]{2,1,0:T(8,128)(2,1)} async-done(((bf16[2,256,128]{2,1,0:T(8,128)(2,1)}), bf16[2,2048,128]{2,1,0:T(8,128)(2,1)}) %all-gather.15.cloned.1.call-update) | async-done | bytes 1048592 | tf_op jit(solution)/shard_map/all_gather | solution.py:76
  99.9 2.6 convolution_bitcast_fusion.43
  112.3 39.2 %psum.42 = f32[64]{0:T(128)S(1)} all-reduce(f32[64]{0:T(128)S(1)} %slice_add_fusion.48), channel_id=1, replica_groups=mesh['sub'=4,'blk'=8] {'sub','blk'}, use_global_device_ids=true, to_apply=%region_2.4 | all-reduce | flops 64 | bytes 512 | tf_op jit(solution)/shard_map/psum | solution.py:91
  153.4 24.0 %all-gather.17.cloned.1.call-done = bf16[2,2048,128]{2,0,1:T(2,128)(2,1)} async-done(((bf16[2,256,128]{2,0,1:T(2,128)(2,1)}), bf16[2,2048,128]{2,0,1:T(2,128)(2,1)}) %all-gather.17.cloned.1.call-update) | async-done | bytes 1048592 | tf_op jit(solution)/shard_map/all_gather | solution.py:72
  177.4 3.3 fusion.57
  189.0 5.4 collective-permute-start.2
  199.0 5.0 collective-permute-done.3
  208.9 24.4 %all-gather.19.cloned.1.call-done = bf16[2,2048,128]{2,1,0:T(8,128)(2,1)} async-done(((bf16[2,256,128]{2,1,0:T(8,128)(2,1)}), bf16[2,2048,128]{2,1,0:T(8,128)(2,1)}) %all-gather.19.cloned.1.call-update) | async-done | bytes 1048592 | tf_op jit(solution)/shard_map/all_gather | solution.py:76
  235.5 2.6 convolution_bitcast_fusion.35
  246.2 39.3 %psum.43 = f32[2,64]{1,0:T(2,128)S(1)} all-reduce(f32[2,64]{1,0:T(2,128)S(1)} %pad_maximum_fusion.8), channel_id=1, replica_groups=mesh['sub'=4,'blk'=8] {'sub','blk'}, use_global_device_ids=true, to_apply=%region_5.7 | all-reduce | flops 128 | bytes 1024 | tf_op jit(solution)/shard_map/psum | solution.py:106
  288.0 23.8 %all-gather.21.cloned.1.call-done = bf16[2,2048,128]{2,0,1:T(2,128)(2,1)} async-done(((bf16[2,256,128]{2,0,1:T(2,128)(2,1)}), bf16[2,2048,128]{2,0,1:T(2,128)(2,1)}) %all-gather.21.cloned.1.call-update) | async-done | bytes 1048592 | tf_op jit(solution)/shard_map/all_gather | solution.py:72
  311.8 3.3 fusion.55
  323.4 5.4 collective-permute-start.4
  334.4 4.0 collective-permute-done.5
  343.3 24.4 %all-gather.23.cloned.1.call-done = bf16[2,2048,128]{2,1,0:T(8,128)(2,1)} async-done(((bf16[2,256,128]{2,1,0:T(8,128)(2,1)}), bf16[2,2048,128]{2,1,0:T(8,128)(2,1)}) %all-gather.23.cloned.1.call-update) | async-done | bytes 1048592 | tf_op jit(solution)/shard_map/all_gather | solution.py:76
  369.9 2.6 convolution_bitcast_fusion.27
  382.4 39.3 %psum.44 = f32[3,64]{1,0:T(4,128)S(1)} all-reduce(f32[3,64]{1,0:T(4,128)S(1)} %pad_maximum_fusion.6), channel_id=1, replica_groups=mesh['sub'=4,'blk'=8] {'sub','blk'}, use_global_device_ids=true, to_apply=%region_9.11 | all-reduce | flops 192 | bytes 1536 | tf_op jit(solution)/shard_map/psum | solution.py:106
  423.9 24.1 %all-gather.25.cloned.1.call-done = bf16[2,2048,128]{2,0,1:T(2,128)(2,1)} async-done(((bf16[2,256,128]{2,0,1:T(2,128)(2,1)}), bf16[2,2048,128]{2,0,1:T(2,128)(2,1)}) %all-gather.25.cloned.1.call-update) | async-done | bytes 1048592 | tf_op jit(solution)/shard_map/all_gather | solution.py:72
  448.0 3.3 fusion.53
  460.3 5.4 collective-permute-start.6
  480.2 24.4 %all-gather.27.cloned.1.call-done = bf16[2,2048,128]{2,1,0:T(8,128)(2,1)} async-done(((bf16[2,256,128]{2,1,0:T(8,128)(2,1)}), bf16[2,2048,128]{2,1,0:T(8,128)(2,1)}) %all-gather.27.cloned.1.call-update) | async-done | bytes 1048592 | tf_op jit(solution)/shard_map/all_gather | solution.py:76
  514.6 2.6 convolution_bitcast_fusion.17
  520.1 39.3 %psum.45 = f32[4,64]{1,0:T(4,128)S(1)} all-reduce(f32[4,64]{1,0:T(4,128)S(1)} %pad_maximum_fusion.7), channel_id=1, replica_groups=mesh['sub'=4,'blk'=8] {'sub','blk'}, use_global_device_ids=true, to_apply=%region_15.17 | all-reduce | flops 256 | bytes 2048 | tf_op jit(solution)/shard_map/psum | solution.py:106
  561.9 24.0 %all-gather.29.cloned.1.call-done = bf16[2,2048,128]{2,0,1:T(2,128)(2,1)} async-done(((bf16[2,256,128]{2,0,1:T(2,128)(2,1)}), bf16[2,2048,128]{2,0,1:T(2,128)(2,1)}) %all-gather.29.cloned.1.call-update) | async-done | bytes 1048592 | tf_op jit(solution)/shard_map/all_gather | solution.py:72
  585.9 3.3 fusion.51
  598.5 5.4 collective-permute-start.8
  618.5 24.4 %all-gather.31.cloned.1.call-done = bf16[2,2048,128]{2,1,0:T(8,128)(2,1)} async-done(((bf16[2,256,128]{2,1,0:T(8,128)(2,1)}), bf16[2,2048,128]{2,1,0:T(8,128)(2,1)}) %all-gather.31.cloned.1.call-update) | async-done | bytes 1048592 | tf_op jit(solution)/shard_map/all_gather | solution.py:76
  647.3 3.3 convolution_bitcast_fusion.11
  652.5 3.3 convolution_bitcast_fusion.8
  657.8 3.3 convolution_bitcast_fusion.9
  665.1 39.3 %psum.46 = f32[5,64]{1,0:T(8,128)S(1)} all-reduce(f32[5,64]{1,0:T(8,128)S(1)} %stack.288), channel_id=1, replica_groups=mesh['sub'=4,'blk'=8] {'sub','blk'}, use_global_device_ids=true, to_apply=%region_22.24 | all-reduce | flops 320 | bytes 2560 | tf_op jit(solution)/shard_map/psum | solution.py:106
  707.6 24.0 %all-gather.33.cloned.1.call-done = bf16[2,2048,128]{2,0,1:T(2,128)(2,1)} async-done(((bf16[2,256,128]{2,0,1:T(2,128)(2,1)}), bf16[2,2048,128]{2,0,1:T(2,128)(2,1)}) %all-gather.33.cloned.1.call-update) | async-done | bytes 1048592 | tf_op jit(solution)/shard_map/all_gather | solution.py:72
  731.6 3.3 fusion.49
  744.2 5.3 collective-permute-start.10
  769.3 19.4 %all-gather.35.cloned.1.call-done = bf16[2,2048,128]{2,1,0:T(8,128)(2,1)} async-done(((bf16[2,256,128]{2,1,0:T(8,128)(2,1)}), bf16[2,2048,128]{2,1,0:T(8,128)(2,1)}) %all-gather.35.cloned.1.call-update) | async-done | bytes 1048592 | tf_op jit(solution)/shard_map/all_gather | solution.py:76
  793.1 3.3 convolution_bitcast_fusion.3
  798.4 3.3 convolution_bitcast_fusion
  803.6 3.3 convolution_bitcast_fusion.1
  811.1 39.3 %psum.47 = f32[6,64]{1,0:T(8,128)S(1)} all-reduce(f32[6,64]{1,0:T(8,128)S(1)} %stack.302), channel_id=1, replica_groups=mesh['sub'=4,'blk'=8] {'sub','blk'}, use_global_device_ids=true, to_apply=%region_30.32 | all-reduce | flops 384 | bytes 3072 | tf_op jit(solution)/shard_map/psum | solution.py:106
  855.9 36.7 %custom-call.11 = f32[64,5,5]{2,1,0:T(8,128)S(1)} custom-call(f32[64,5,5]{2,1,0:T(8,128)} %fusion.6), custom_call_target="Cholesky" | custom-call | tf_op jit(solution)/shard_map/jit(cholesky)/cholesky | solution.py:119
  (444 shorter events, 220.9 us)
Async XLA Ops:
  6.5 34.9 %copy-start = (bf16[1,2,256,2048]{3,2,1,0:T(8,128)(2,1)S(1)}, bf16[1,2,256,2048]{3,2,1,0:T(8,128)(2,1)}, u32[]{:S(2)}) copy-start(bf16[1,2,256,2048]{3,2,1,0:T(8,128)(2,1)} %param.15) | copy-start | bytes 6291460
  6.5 28.8 %all-gather.13.cloned.1.call-start = ((), (), s32[]{:S(2)}) async-start(), calls=%async_computation | async-start | bytes 1179648 | tf_op jit(solution)/shard_map/all_gather | solution.py:72
  7.9 31.6 %copy-start.24 = (f32[2,256,64]{2,1,0:T(8,128)}, f32[2,256,64]{2,1,0:T(8,128)S(1)}, u32[]{:S(2)}) copy-start(f32[2,256,64]{2,1,0:T(8,128)S(1)} %get-tuple-element.68) | copy-start | bytes 393220
  7.9 31.6 %copy-start.25 = (f32[2,256,64]{2,1,0:T(8,128)}, f32[2,256,64]{2,1,0:T(8,128)S(1)}, u32[]{:S(2)}) copy-start(f32[2,256,64]{2,1,0:T(8,128)S(1)} %get-tuple-element.69) | copy-start | bytes 393220
  8.8 88.9 %all-gather.15.cloned.1.call-start = ((), (), s32[]{:S(2)}) async-start(), calls=%async_computation.1 | async-start | bytes 1179648 | tf_op jit(solution)/shard_map/all_gather | solution.py:76
  14.8 53.3 %copy-start.32 = (s32[1024]{0:T(1024)}, s32[1024]{0:T(1024)S(1)}, u32[]{:S(2)}) copy-start(s32[1024]{0:T(1024)S(1)} %pad_clamp_fusion) | copy-start | bytes 12292
  14.9 600.6 %copy-start.31 = (s32[1024]{0:T(1024)}, s32[1024]{0:T(1024)S(1)}, u32[]{:S(2)}) copy-start(s32[1024]{0:T(1024)S(1)} %pad_clamp_fusion.1) | copy-start | bytes 12292
  35.4 5.0 copy-start.1
  52.1 16.0 %collective-permute-start.1 = (bf16[2,1024,128]{2,0,1:T(2,128)(2,1)S(1)}, bf16[2,1024,128]{2,0,1:T(2,128)(2,1)}, u32[]{:S(2)}, u32[]{:S(2)}) collective-permute-start(bf16[2,1024,128]{2,0,1:T(2,128)(2,1)S(1)} %get-tuple-element.63), channel_id=1, source_target_pairs={{8,0},{16,8},{24,16},{9,1},{17,9},{25,17},{10,2},{18,10},{26,18},{... | collective-permute-start | bytes 1572872 | tf_op jit(solution)/shard_map/ppermute | solution.py:15
  53.4 16.6 %collective-permute-start = (bf16[2,1024,128]{2,0,1:T(2,128)(2,1)}, bf16[2,1024,128]{2,0,1:T(2,128)(2,1)}, u32[]{:S(2)}, u32[]{:S(2)}) collective-permute-start(bf16[2,1024,128]{2,0,1:T(2,128)(2,1)} %get-tuple-element.62), channel_id=1, source_target_pairs={{0,8},{8,16},{16,24},{1,9},{9,17},{17,25},{2,10},{10,18},{18,26},{... | collective-permute-start | bytes 1572872 | tf_op jit(solution)/shard_map/ppermute | solution.py:15
  59.0 13.2 %copy-start.29 = (f32[2]{0:T(128)S(1)}, f32[2]{0:T(128)}, u32[]{:S(2)}) copy-start(f32[2]{0:T(128)} %constant.128.clone) | copy-start | bytes 28
  73.0 104.4 %all-gather.17.cloned.1.call-start = ((), (), s32[]{:S(2)}) async-start(), calls=%async_computation.2 | async-start | bytes 1179648 | tf_op jit(solution)/shard_map/all_gather | solution.py:72
  153.2 80.2 %all-gather.19.cloned.1.call-start = ((), (), s32[]{:S(2)}) async-start(), calls=%async_computation.3 | async-start | bytes 1179648 | tf_op jit(solution)/shard_map/all_gather | solution.py:76
  177.4 3.3 copy-start.2
  180.7 1.6 copy-start.7
  183.2 1.6 copy-start.12
  187.7 16.3 %collective-permute-start.3 = (bf16[2,1024,128]{2,0,1:T(2,128)(2,1)}, bf16[2,1024,128]{2,0,1:T(2,128)(2,1)}, u32[]{:S(2)}, u32[]{:S(2)}) collective-permute-start(bf16[2,1024,128]{2,0,1:T(2,128)(2,1)} %get-tuple-element.59), channel_id=1, source_target_pairs={{8,0},{16,8},{24,16},{9,1},{17,9},{25,17},{10,2},{18,10},{26,18},{... | collective-permute-start | bytes 1572872 | tf_op jit(solution)/shard_map/ppermute | solution.py:15
  189.0 17.0 %collective-permute-start.2 = (bf16[2,1024,128]{2,0,1:T(2,128)(2,1)}, bf16[2,1024,128]{2,0,1:T(2,128)(2,1)}, u32[]{:S(2)}, u32[]{:S(2)}) collective-permute-start(bf16[2,1024,128]{2,0,1:T(2,128)(2,1)} %get-tuple-element.58), channel_id=1, source_target_pairs={{0,8},{8,16},{16,24},{1,9},{9,17},{17,25},{2,10},{10,18},{18,26},{... | collective-permute-start | bytes 1572872 | tf_op jit(solution)/shard_map/ppermute | solution.py:15
  208.9 102.9 %all-gather.21.cloned.1.call-start = ((), (), s32[]{:S(2)}) async-start(), calls=%async_computation.4 | async-start | bytes 1179648 | tf_op jit(solution)/shard_map/all_gather | solution.py:72
  287.5 80.2 %all-gather.23.cloned.1.call-start = ((), (), s32[]{:S(2)}) async-start(), calls=%async_computation.5 | async-start | bytes 1179648 | tf_op jit(solution)/shard_map/all_gather | solution.py:76
  311.8 3.3 copy-start.3
  315.1 1.6 copy-start.8
  317.6 1.6 copy-start.13
  322.1 16.3 %collective-permute-start.5 = (bf16[2,1024,128]{2,0,1:T(2,128)(2,1)}, bf16[2,1024,128]{2,0,1:T(2,128)(2,1)}, u32[]{:S(2)}, u32[]{:S(2)}) collective-permute-start(bf16[2,1024,128]{2,0,1:T(2,128)(2,1)} %get-tuple-element.55), channel_id=1, source_target_pairs={{8,0},{16,8},{24,16},{9,1},{17,9},{25,17},{10,2},{18,10},{26,18},{... | collective-permute-start | bytes 1572872 | tf_op jit(solution)/shard_map/ppermute | solution.py:15
  323.4 17.0 %collective-permute-start.4 = (bf16[2,1024,128]{2,0,1:T(2,128)(2,1)}, bf16[2,1024,128]{2,0,1:T(2,128)(2,1)}, u32[]{:S(2)}, u32[]{:S(2)}) collective-permute-start(bf16[2,1024,128]{2,0,1:T(2,128)(2,1)} %get-tuple-element.54), channel_id=1, source_target_pairs={{0,8},{8,16},{16,24},{1,9},{9,17},{17,25},{2,10},{10,18},{18,26},{... | collective-permute-start | bytes 1572872 | tf_op jit(solution)/shard_map/ppermute | solution.py:15
  343.3 104.7 %all-gather.25.cloned.1.call-start = ((), (), s32[]{:S(2)}) async-start(), calls=%async_computation.6 | async-start | bytes 1179648 | tf_op jit(solution)/shard_map/all_gather | solution.py:72
  423.7 80.9 %all-gather.27.cloned.1.call-start = ((), (), s32[]{:S(2)}) async-start(), calls=%async_computation.7 | async-start | bytes 1179648 | tf_op jit(solution)/shard_map/all_gather | solution.py:76
  448.0 3.3 copy-start.4
  451.3 1.6 copy-start.9
  459.0 16.3 %collective-permute-start.7 = (bf16[2,1024,128]{2,0,1:T(2,128)(2,1)}, bf16[2,1024,128]{2,0,1:T(2,128)(2,1)}, u32[]{:S(2)}, u32[]{:S(2)}) collective-permute-start(bf16[2,1024,128]{2,0,1:T(2,128)(2,1)} %get-tuple-element.51), channel_id=1, source_target_pairs={{8,0},{16,8},{24,16},{9,1},{17,9},{25,17},{10,2},{18,10},{26,18},{... | collective-permute-start | bytes 1572872 | tf_op jit(solution)/shard_map/ppermute | solution.py:15
  460.3 17.0 %collective-permute-start.6 = (bf16[2,1024,128]{2,0,1:T(2,128)(2,1)}, bf16[2,1024,128]{2,0,1:T(2,128)(2,1)}, u32[]{:S(2)}, u32[]{:S(2)}) collective-permute-start(bf16[2,1024,128]{2,0,1:T(2,128)(2,1)} %get-tuple-element.50), channel_id=1, source_target_pairs={{0,8},{8,16},{16,24},{1,9},{9,17},{17,25},{2,10},{10,18},{18,26},{... | collective-permute-start | bytes 1572872 | tf_op jit(solution)/shard_map/ppermute | solution.py:15
  480.2 105.7 %all-gather.29.cloned.1.call-start = ((), (), s32[]{:S(2)}) async-start(), calls=%async_computation.8 | async-start | bytes 1179648 | tf_op jit(solution)/shard_map/all_gather | solution.py:72
  559.5 29.8 %copy-start.30 = (f32[4,64]{1,0:T(4,128)}, f32[4,64]{1,0:T(4,128)S(1)}, u32[]{:S(2)}) copy-start(f32[4,64]{1,0:T(4,128)S(1)} %psum.45) | copy-start | bytes 3076
  561.6 81.3 %all-gather.31.cloned.1.call-start = ((), (), s32[]{:S(2)}) async-start(), calls=%async_computation.9 | async-start | bytes 1179648 | tf_op jit(solution)/shard_map/all_gather | solution.py:76
  585.9 3.3 copy-start.5
  589.2 1.6 copy-start.10
  597.2 16.3 %collective-permute-start.9 = (bf16[2,1024,128]{2,0,1:T(2,128)(2,1)}, bf16[2,1024,128]{2,0,1:T(2,128)(2,1)}, u32[]{:S(2)}, u32[]{:S(2)}) collective-permute-start(bf16[2,1024,128]{2,0,1:T(2,128)(2,1)} %get-tuple-element.47), channel_id=1, source_target_pairs={{8,0},{16,8},{24,16},{9,1},{17,9},{25,17},{10,2},{18,10},{26,18},{... | collective-permute-start | bytes 1572872 | tf_op jit(solution)/shard_map/ppermute | solution.py:15
  598.5 17.0 %collective-permute-start.8 = (bf16[2,1024,128]{2,0,1:T(2,128)(2,1)}, bf16[2,1024,128]{2,0,1:T(2,128)(2,1)}, u32[]{:S(2)}, u32[]{:S(2)}) collective-permute-start(bf16[2,1024,128]{2,0,1:T(2,128)(2,1)} %get-tuple-element.46), channel_id=1, source_target_pairs={{0,8},{8,16},{16,24},{1,9},{9,17},{17,25},{2,10},{10,18},{18,26},{... | collective-permute-start | bytes 1572872 | tf_op jit(solution)/shard_map/ppermute | solution.py:15
  618.4 113.2 %all-gather.33.cloned.1.call-start = ((), (), s32[]{:S(2)}) async-start(), calls=%async_computation.10 | async-start | bytes 1179648 | tf_op jit(solution)/shard_map/all_gather | solution.py:72
  707.3 81.4 %all-gather.35.cloned.1.call-start = ((), (), s32[]{:S(2)}) async-start(), calls=%async_computation.11 | async-start | bytes 1179648 | tf_op jit(solution)/shard_map/all_gather | solution.py:76
  731.6 3.3 copy-start.6
  734.9 1.6 copy-start.11
  742.9 16.3 %collective-permute-start.11 = (bf16[2,1024,128]{2,0,1:T(2,128)(2,1)}, bf16[2,1024,128]{2,0,1:T(2,128)(2,1)}, u32[]{:S(2)}, u32[]{:S(2)}) collective-permute-start(bf16[2,1024,128]{2,0,1:T(2,128)(2,1)} %get-tuple-element.43), channel_id=1, source_target_pairs={{8,0},{16,8},{24,16},{9,1},{17,9},{25,17},{10,2},{18,10},{26,18},{... | collective-permute-start | bytes 1572872 | tf_op jit(solution)/shard_map/ppermute | solution.py:15
  744.2 17.0 %collective-permute-start.10 = (bf16[2,1024,128]{2,0,1:T(2,128)(2,1)}, bf16[2,1024,128]{2,0,1:T(2,128)(2,1)}, u32[]{:S(2)}, u32[]{:S(2)}) collective-permute-start(bf16[2,1024,128]{2,0,1:T(2,128)(2,1)} %get-tuple-element.42), channel_id=1, source_target_pairs={{0,8},{8,16},{16,24},{1,9},{9,17},{17,25},{2,10},{10,18},{18,26},{... | collective-permute-start | bytes 1572872 | tf_op jit(solution)/shard_map/ppermute | solution.py:15
  769.2 19.5 %copy-start.27 = (f32[64,6,5]{0,1,2:T(8,128)}, f32[64,6,5]{0,1,2:T(8,128)S(1)}, u32[]{:S(2)}) copy-start(f32[64,6,5]{0,1,2:T(8,128)S(1)} %constant_dynamic-update-slice_fusion.1) | copy-start | bytes 23044
  808.0 2.5 copy-start.23
  808.0 43.3 %copy-start.36 = (f32[64]{0:T(128)S(1)}, f32[64]{0:T(128)}, u32[]{:S(2)}) copy-start(f32[64]{0:T(128)} %copy-done.35) | copy-start | bytes 772
  808.1 42.3 %copy-start.28 = (f32[64,6,5]{0,1,2:T(8,128)S(1)}, f32[64,6,5]{0,1,2:T(8,128)}, u32[]{:S(2)}) copy-start(f32[64,6,5]{0,1,2:T(8,128)} %copy-done.27) | copy-start | bytes 23044
  (16 other events, 17.3 us)
Sparse Core Ops, SparseCore 0:
  9.2 26.1 all-gather.12
  73.1 24.6 all-gather.14
  153.3 24.0 all-gather.16
  209.0 24.2 all-gather.18
  287.6 24.1 all-gather.20
  343.4 24.2 all-gather.22
  423.8 24.1 all-gather.24
  480.3 24.2 all-gather.26
  561.7 24.1 all-gather.28
  618.6 24.2 all-gather.30
  707.4 24.1 all-gather.32
  764.4 24.2 all-gather.34
where the time goes:
time: 917 us; the launch traced here: 903 us
  waiting for transfers between devices  301 us (33%)
  blocking collectives  236 us (26%)
  other arithmetic  107 us (12%)
  local copies, waits for them, and re-layouts  102 us (11%)
  matrix products  100 us (11%)
  starting transfers between devices  41.6 us (5%)
  between operations  15.8 us (2%)
    psum x5, blocking collectives, body(): summed = lax.psum(stacked_dots, ('sub', 'blk'))  197 us
    all_gather x6, waiting for transfers between devices, preconditioned(): middle_full = lax.all_gather(middle_rounded, 'blk', axis=1, tiled=True)  141 us
    all_gather x6, waiting for transfers between devices, preconditioned(): gathered = lax.all_gather(rounded, 'blk', axis=1, tiled=True)  140 us
    dot_general x48, matrix products, complex_product(): jnp.dot(matrix.reshape(2 * count, matrix.shape[2]), vector, preferred_ele...  98.6 us
    ppermute x12, starting transfers between devices, passed_along(): return lax.ppermute(block, axis, route)  39.9 us
    psum x1, blocking collectives, global_norm(): lax.psum(inner_local(vector, vector), ('sub', 'blk')) + EPSILON  39.2 us
    another operation x4, other arithmetic, body(): factor = jnp.linalg.cholesky(gram)  36.8 us
    sub x46, other arithmetic, complex_product(): real_part = products[0, :, :width] - products[1, :, width:]  25 us
  transfers between devices with their start and end apart: 24, of which 18 were waited for; matrix products, arithmetic and copies ran while one was open for 7% of the time, Pallas kernels for 0%

commit v1 on v0

v1 whole, which is shorter than its diff:
```python
import functools

import jax
import jax.numpy as jnp
from jax import lax
from jax.experimental import pallas as pl
from jax.experimental.pallas import tpu as pltpu
from jax.sharding import PartitionSpec as P

BASIS = 5
EPSILON = 1e-06
MESH = pl.DeviceIdType.MESH


def mm(a, b):
    return jnp.dot(a, b, preferred_element_type=jnp.float32)


def swap(x):
    width = x.shape[-1] // 2
    return jnp.concatenate([x[..., width:], x[..., :width]], axis=-1)


def turned(x):
    width = x.shape[-1] // 2
    return jnp.concatenate([-x[..., width:], x[..., :width]], axis=-1)


def kernel(ns, n, paired, dl, sl, hy, ad, up, down, rhs, start, out,
           buf, acc, sel, spread_sel, xs, xr, y, img, basis, coef, red1, red2,
           gsend, grecv, xsend, xrecv, r1send, r1recv, r2send, r2recv):
    s = lax.axis_index("sub")
    b = lax.axis_index("blk")
    rows = rhs.shape[3]
    total = dl.shape[3]
    half = rows // 2
    nq = n // 2 if paired else n
    chunked = rows % 128 == 0

    def blk_peer(k):
        return lax.rem(b + k, n)

    def sub_peer(k):
        return lax.rem(s + k, ns)

    def flat(ref, t):
        return jnp.concatenate([ref[0, t, 0], ref[0, t, 1]], axis=-1)

    lane = lax.broadcasted_iota(jnp.int32, (half, total), 1)
    line = lax.broadcasted_iota(jnp.int32, (half, total), 0)
    sel[pl.ds(0, half)] = jnp.where(lane == up[...], 1.0, 0.0).astype(jnp.bfloat16)
    sel[pl.ds(half, half)] = jnp.where(line == down[...], 1.0, 0.0).astype(jnp.bfloat16)
    r_at = lax.broadcasted_iota(jnp.int32, (rows, rows), 0)
    m_at = lax.broadcasted_iota(jnp.int32, (rows, rows), 1)
    goes = jnp.where(m_at < half, 2 * m_at, 2 * (m_at - half) + 1)
    spread_sel[...] = jnp.where(r_at == goes, 1.0, 0.0).astype(jnp.bfloat16)
    xr[...] = jnp.zeros_like(xr)
    basis[...] = jnp.zeros_like(basis)
    own = pl.ds(pl.multiple_of(b * rows, rows), rows)
    for t in range(2):
        buf[0, t, own, :] = flat(start, t).astype(jnp.bfloat16)

    barrier = pltpu.get_barrier_semaphore()
    for k in range(1, n):
        pl.semaphore_signal(barrier, inc=1, device_id=(s, blk_peer(k)), device_id_type=MESH)
    for k in range(1, ns):
        pl.semaphore_signal(barrier, inc=1, device_id=(sub_peer(k), b), device_id_type=MESH)
    pl.semaphore_wait(barrier, n - 1 + ns - 1)

    def block_of(owner):
        return pl.ds(pl.multiple_of(owner * rows, rows), rows)

    def send(g, owner, to, at):
        piece = buf.at[g, :, block_of(owner), :]
        return pltpu.make_async_remote_copy(
            src_ref=piece, dst_ref=piece, send_sem=gsend.at[g, at], recv_sem=grecv.at[g, at],
            device_id=(s, to), device_id_type=MESH)

    def gather(g, arrived):
        if paired:
            q, c = b // 2, lax.rem(b, 2)
            mate = 2 * q + 1 - c
            sends = [send(g, b, 2 * lax.rem(q + k, nq) + c, k) for k in range(1, nq)]
            for one in sends:
                one.start()
            mine = send(g, b, mate, nq)
            mine.start()
            sends.append(mine)
            arrived(0, b)
            mine.wait_recv()
            arrived(1, mate)
            count = 2
            for k in range(1, nq):
                sends[k - 1].wait_recv()
                far = lax.rem(q - k + nq, nq)
                on = send(g, 2 * far + c, mate, nq + k)
                on.start()
                sends.append(on)
                arrived(count, 2 * far + c)
                on.wait_recv()
                arrived(count + 1, 2 * far + 1 - c)
                count += 2
        else:
            sends = [send(g, b, blk_peer(k), k) for k in range(1, n)]
            for one in sends:
                one.start()
            arrived(0, b)
            for k in range(1, n):
                sends[k - 1].wait_recv()
                arrived(k, lax.rem(b - k + n, n))
        return sends

    def accumulate(g, where, first):
        d, m = buf[g, 0, where, :], buf[g, 1, where, :]
        for p in range(2):
            top = mm(sl[0, p, :, where], m) - mm(dl[0, p, :, where], d)
            low = mm(hy[0, p, :, where], d) + mm(ad[0, p, :, where], m)
            acc[p] = top if first else acc[p] + top
            acc[2 + p] = low if first else acc[2 + p] + low

    def pick(where, first):
        width = buf.shape[3]
        for t in range(2):
            part = mm(sel[:, where], buf[0, t, where, :])
            at = pl.ds(t * width, width)
            y[:, at] = part if first else y[:, at] + part

    everything = pl.ds(0, total)

    def couple(k_dir):
        to = s + 1 if k_dir == 0 else s - 1
        piece = pl.ds(k_dir * half, half)
        return pltpu.make_async_remote_copy(
            src_ref=xs.at[piece], dst_ref=xr.at[piece], send_sem=xsend.at[k_dir],
            recv_sem=xrecv.at[k_dir], device_id=(to, b), device_id_type=MESH)

    def step(k, carry):
        held = []

        def first_arrival(count, owner):
            where = block_of(owner)
            if chunked:
                pick(where, count == 0)
                if count < n // 2:
                    accumulate(0, where, count == 0)
                else:
                    held.append(where)

        sends = gather(0, first_arrival)
        if not chunked:
            pick(everything, True)
        xs[...] = y[...].astype(jnp.bfloat16)

        @pl.when(s < ns - 1)
        def _():
            couple(0).start()

        @pl.when(s > 0)
        def _():
            couple(1).start()

        for where in held:
            accumulate(0, where, False)
        if not chunked:
            accumulate(0, everything, True)
        for one in sends:
            one.wait_send()

        @pl.when(s < ns - 1)
        def _():
            couple(0).wait_send()
            couple(1).wait_recv()

        @pl.when(s > 0)
        def _():
            couple(1).wait_send()
            couple(0).wait_recv()

        coupled = mm(spread_sel[...], xr[...])
        width = buf.shape[3]
        for t in range(2):
            sign = -0.5 if t == 0 else 0.5
            middle = acc[2 * t] + turned(acc[2 * t + 1]) + sign * coupled[:, t * width:(t + 1) * width]
            buf[1, t, own, :] = middle.astype(jnp.bfloat16)

        def second_arrival(count, owner):
            if chunked:
                accumulate(1, block_of(owner), count == 0)

        sends = gather(1, second_arrival)
        if not chunked:
            accumulate(1, everything, True)
        for t in range(2):
            image = acc[2 * t] + turned(acc[2 * t + 1])
            img[t] = jnp.where(k == 0, flat(rhs, t) - image, image)

        par = lax.rem(k, 2)
        dots = [jnp.sum(basis[i] * img[...], axis=(0, 1))[None] for i in range(BASIS)]
        dots.append(jnp.sum(img[...] * img[...], axis=(0, 1))[None])
        dots.append(jnp.zeros((2, dots[0].shape[1]), jnp.float32))
        red1[par, b] = jnp.concatenate(dots, axis=0)
        moves = []
        for d in range(1, n):
            one = pltpu.make_async_remote_copy(
                src_ref=red1.at[par, b], dst_ref=red1.at[par, b], send_sem=r1send.at[par, d],
                recv_sem=r1recv.at[par, d], device_id=(s, blk_peer(d)), device_id_type=MESH)
            one.start()
            moves.append(one)
        for one in sends:
            one.wait_send()
        for one in moves:
            one.wait()
        red2[par, s] = jnp.sum(red1[par], axis=0)
        moves = []
        for d in range(1, ns):
            one = pltpu.make_async_remote_copy(
                src_ref=red2.at[par, s], dst_ref=red2.at[par, s], send_sem=r2send.at[par, d],
                recv_sem=r2recv.at[par, d], device_id=(sub_peer(d), b), device_id_type=MESH)
            one.start()
            moves.append(one)
        for one in moves:
            one.wait()
        summed = jnp.sum(red2[par], axis=0)
        summed = summed + swap(summed)
        squares = summed[BASIS:BASIS + 1]
        for i in range(BASIS):
            squares = squares - summed[i:i + 1] * summed[i:i + 1]
        height = jnp.sqrt(jnp.maximum(squares, 0.0) + EPSILON)
        coef[k] = jnp.concatenate([summed[:BASIS], height, jnp.zeros((2, height.shape[1]), jnp.float32)], axis=0)
        scale = 1.0 / height
        for t in range(2):
            w = img[t]
            for i in range(BASIS):
                w = w - summed[i:i + 1] * basis[i, t]
            w = w * scale
            basis[k, t] = w
            buf[0, t, own, :] = w.astype(jnp.bfloat16)
        return carry

    lax.fori_loop(0, BASIS + 1, step, 0)

    table = [coef[k] for k in range(BASIS + 1)]
    beta = table[0][BASIS:BASIS + 1]

    def entry(i, j):
        return table[j + 1][i:i + 1] if i <= j else table[j + 1][BASIS:BASIS + 1]

    low = [[None] * BASIS for _ in range(BASIS)]
    mid = []
    for j in range(BASIS):
        for l in range(j, BASIS):
            gram = sum(entry(i, j) * entry(i, l) for i in range(j + 2))
            for m in range(j):
                gram = gram - low[j][m] * low[l][m]
            if l == j:
                low[j][j] = jnp.sqrt(gram)
            else:
                low[l][j] = gram / low[j][j]
    for j in range(BASIS):
        value = beta * entry(0, j)
        for m in range(j):
            value = value - low[j][m] * mid[m]
        mid.append(value / low[j][j])
    z = [None] * BASIS
    for j in reversed(range(BASIS)):
        value = mid[j]
        for m in range(j + 1, BASIS):
            value = value - low[m][j] * z[m]
        z[j] = value / low[j][j]
    for t in range(2):
        result = flat(start, t)
        for j in range(BASIS):
            result = result + z[j] * basis[j, t]
        out[t] = result


def body(ns, n, paired, double_layer, single_layer, hypersingular, adjoint_double, matching, right_side, start):
    rows, total = double_layer.shape[2:]
    width = 2 * right_side.shape[4]
    half = rows // 2
    s = lax.axis_index("sub")
    window = lax.axis_index("blk") * half
    above = lax.dynamic_slice(matching, (jnp.minimum(s + 1, ns - 1), window), (1, half))
    up = jnp.where(s < ns - 1, 2 * above + 1, -1).reshape(half, 1)
    here = lax.dynamic_slice(matching, (s, 0), (1, matching.shape[1]))
    here = jnp.where(s > 0, here - window, -1)
    down = jnp.stack([here, jnp.full_like(here, -1)], axis=2).reshape(1, total)
    dma = pltpu.SemaphoreType.DMA
    vmem = pl.BlockSpec(memory_space=pltpu.VMEM)
    out = pl.pallas_call(
        functools.partial(kernel, ns, n, paired),
        out_shape=jax.ShapeDtypeStruct((2, rows, width), jnp.float32),
        in_specs=[vmem] * 8,
        out_specs=vmem,
        scratch_shapes=[
            pltpu.VMEM((2, 2, total, width), jnp.bfloat16),
            pltpu.VMEM((4, rows, width), jnp.float32),
            pltpu.VMEM((rows, total), jnp.bfloat16),
            pltpu.VMEM((rows, rows), jnp.bfloat16),
            pltpu.VMEM((rows, 2 * width), jnp.bfloat16),
            pltpu.VMEM((rows, 2 * width), jnp.bfloat16),
            pltpu.VMEM((rows, 2 * width), jnp.float32),
            pltpu.VMEM((2, rows, width), jnp.float32),
            pltpu.VMEM((BASIS + 1, 2, rows, width), jnp.float32),
            pltpu.VMEM((BASIS + 1, 8, width), jnp.float32),
            pltpu.VMEM((2, n, 8, width), jnp.float32),
            pltpu.VMEM((2, ns, 8, width), jnp.float32),
            dma((2, n)), dma((2, n)), dma((2,)), dma((2,)),
            dma((2, n)), dma((2, n)), dma((2, ns)), dma((2, ns)),
        ],
        compiler_params=pltpu.CompilerParams(
            collective_id=0, has_side_effects=True, vmem_limit_bytes=48 * 1024 * 1024),
    )(double_layer, single_layer, hypersingular, adjoint_double, up, down, right_side, start)
    half_width = width // 2
    return jnp.stack([out[..., :half_width], out[..., half_width:]], axis=1)[None]


def chip_pairs(mesh):
    lines = mesh.devices.reshape(mesh.shape["sub"], mesh.shape["blk"])
    if lines.shape[1] % 2:
        return False
    spots = [[tuple(getattr(d, "coords", None) or (d.id,)) for d in line] for line in lines]
    return all(line[i] == line[i + 1] for line in spots for i in range(0, len(line), 2))


def solution(mesh):
    placed = (
        P("sub", None, "blk", None),
        P("sub", None, "blk", None),
        P("sub", None, "blk", None),
        P("sub", None, "blk", None),
        P(),
        P("sub", None, None, "blk", None),
        P("sub", None, None, "blk", None),
    )
    return jax.shard_map(
        functools.partial(body, mesh.shape["sub"], mesh.shape["blk"], chip_pairs(mesh)),
        mesh=mesh,
        in_specs=placed,
        out_specs=P("sub", None, None, "blk", None),
        check_vma=False,
    )
```

time: 917 us -> 197 us (0.21); the launches traced: 903 us -> 196 us
  waiting for transfers between devices: 301 us -> 0 us
  blocking collectives: 236 us -> 0 us
  Pallas kernels: 0 us -> 190 us
  other arithmetic: 107 us -> 1.67 us
  matrix products: 100 us -> 0 us
  local copies, waits for them, and re-layouts: 102 us -> 4.63 us
  starting transfers between devices: 41.6 us -> 0 us
  between operations: 15.8 us -> 0.09 us
    all_gather x12 -> x0, waiting for transfers between devices: 281 us -> none  [the longest x6 141 us: preconditioned(): middle_full = lax.all_gather(middle_rounded, 'blk', axis=1, tiled=True)]
    psum x6 -> x0, blocking collectives: 236 us -> none  [the longest x5 197 us: body(): summed = lax.psum(stacked_dots, ('sub', 'blk'))]
    pallas_call x0 -> x1, Pallas kernels: none -> 190 us  [body(): pl.pallas_call(functools.partial(kernel, ns, n, paired), out_shape=jax.Sh...]
    dot_general x49 -> x0, matrix products: 100 us -> none  [the longest x48 98.6 us: complex_product(): jnp.dot(matrix.reshape(2 * count, matrix.shape[2]), vector, preferred_ele...]
    ppermute x12 -> x0, starting transfers between devices: 39.9 us -> none  [passed_along(): return lax.ppermute(block, axis, route)]
    another operation x44 -> x1, other arithmetic: 40.3 us -> 0.73 us  [body(): down = jnp.stack([here, jnp.full_like(here, -1)], axis=2).reshape(1, total)]
    sub x58 -> x0, other arithmetic: 36.8 us -> none  [the longest x46 25 us: complex_product(): real_part = products[0, :, :width] - products[1, :, width:]]
    slice x13 -> x0, local copies, waits for them, and re-layouts: 31.9 us -> none  [the longest x6 20.6 us: calderon(): vector[1]]
  transfers between devices with their start and end apart: 24 -> 0, of which waited for: 18 -> 0; matrix products, arithmetic and copies ran while one was open for 7% -> 0% of each run, Pallas kernels for 0% -> 0%
where the time goes in v1:
time: 197 us; the launch traced here: 196 us
  Pallas kernels  190 us (96%)
  local copies, waits for them, and re-layouts  4.63 us (2%)
    pallas_call x1, Pallas kernels, body(): pl.pallas_call(functools.partial(kernel, ns, n, paired), out_shape=jax.Sh...  190 us

profile of v1, /device:TPU:0, one launch (start us, length us, event | category | flops | bytes accessed | tf_op | source)
XLA Modules:
  0.0 196.4 jit_solution(16600906466402168771)
XLA Ops:
  0.0 0.0 copy-start.2
  0.0 0.0 copy-start
  0.0 0.9 fusion.1
  0.9 0.7 fusion
  1.6 0.1 copy.13.up
  1.8 0.2 copy.17
  2.0 0.3 reshape.7.down
  2.3 0.0 copy-done.2
  2.4 0.2 copy.14.rhs
  2.6 1.1 copy.15.start
  3.7 0.0 copy-done
  3.7 0.0 copy-start.1
  3.7 1.6 copy-done.1
  5.3 190.0 %shard_map.73 = f32[2,256,128]{2,1,0:T(8,128)S(1)} custom-call(bf16[1,2,256,2048]{3,2,1,0:T(8,128)(2,1)S(1)} %copy-done, bf16[1,2,256,2048]{3,2,1,0:T(8,128)(2,1)S(1)} %copy-done.1, bf16[1,2,256,2048]{3,2,1,0:T(8,128)(2,1)} %hy.1, bf16[1,2,256,2048]{3,2,1,0:T(8,128)(2,1)} %ad.1, s32[128,1]{1,0:T(8,128)S(1)} %copy.13.up, s32[1,2048]{1,0:T(1,128)S(1)} %reshape.7.down, ...), custom_call_target="tpu_custom_call" | custom-call | tf_op jit(solution)/shard_map/pallas_call | solution.py:290
  195.3 0.1 slice_bitcast_fusion.1
  195.5 0.9 copy.16
  (2 shorter events, 0.1 us)
Async XLA Ops:
  0.0 2.3 %copy-start.2 = (f32[1,2,2,256,64]{3,4,2,1,0:T(8,128)S(1)}, f32[1,2,2,256,64]{3,4,2,1,0:T(8,128)}, u32[]{:S(2)}) copy-start(f32[1,2,2,256,64]{3,4,2,1,0:T(8,128)} %param.12) | copy-start | bytes 786436
  0.0 3.7 %copy-start = (bf16[1,2,256,2048]{3,2,1,0:T(8,128)(2,1)S(1)}, bf16[1,2,256,2048]{3,2,1,0:T(8,128)(2,1)}, u32[]{:S(2)}) copy-start(bf16[1,2,256,2048]{3,2,1,0:T(8,128)(2,1)} %dl.1) | copy-start | bytes 6291460
  3.7 1.6 copy-start.1

commit v2 on v1

--- a/solution.py
+++ b/solution.py
@@ -26,13 +26,13 @@
     return jnp.concatenate([-x[..., width:], x[..., :width]], axis=-1)
 
 
-def kernel(ns, n, paired, dl, sl, hy, ad, up, down, rhs, start, out,
-           buf, acc, sel, spread_sel, xs, xr, y, img, basis, coef, red1, red2,
-           gsend, grecv, xsend, xrecv, r1send, r1recv, r2send, r2recv):
+def kernel(ns, n, paired, dl_in, sl_in, hy_in, ad_in, up, down, rhs, start, out,
+           dl, sl, hy, ad, buf, acc, sel, spread_sel, xs, xr, y, img, basis, coef, red1, red2,
+           gsend, grecv, xsend, xrecv, r1send, r1recv, r2send, r2recv, load_sem):
     s = lax.axis_index("sub")
     b = lax.axis_index("blk")
     rows = rhs.shape[3]
-    total = dl.shape[3]
+    total = dl_in.shape[3]
     half = rows // 2
     nq = n // 2 if paired else n
     chunked = rows % 128 == 0
@@ -42,6 +42,11 @@
 
     def sub_peer(k):
         return lax.rem(s + k, ns)
+
+    loads = [pltpu.make_async_copy(src.at[0], dst, load_sem.at[i])
+             for i, (src, dst) in enumerate(((dl_in, dl), (sl_in, sl), (hy_in, hy), (ad_in, ad)))]
+    for one in loads:
+        one.start()
 
     def flat(ref, t):
         return jnp.concatenate([ref[0, t, 0], ref[0, t, 1]], axis=-1)
@@ -76,7 +81,67 @@
             src_ref=piece, dst_ref=piece, send_sem=gsend.at[g, at], recv_sem=grecv.at[g, at],
             device_id=(s, to), device_id_type=MESH)
 
-    def gather(g, arrived):
+    def square(g, arrived, ready):
+        q, c = b // 2, lax.rem(b, 2)
+        along_x = 2 * (q // 2) + 1 - lax.rem(q, 2)
+        along_y = lax.rem(q + 2, 4)
+        near = along_x + c * (along_y - along_x)
+        side = along_y + c * (along_x - along_y)
+        diagonal = 3 - q
+        mate = 2 * q + 1 - c
+
+        def go(kind, piece, owner, to):
+            lines = pl.ds(pl.multiple_of(owner * rows + piece % 2 * half, half), half)
+            part = buf.at[g, piece // 2, lines, :]
+            at = 4 * kind + piece
+            one = pltpu.make_async_remote_copy(
+                src_ref=part, dst_ref=part, send_sem=gsend.at[g, at], recv_sem=grecv.at[g, at],
+                device_id=(s, to), device_id_type=MESH)
+            sent[kind, piece] = one
+            one.start()
+
+        sent = {}
+        pieces = range(4)
+        for t in range(2):
+            ready(t)
+            for p in (2 * t, 2 * t + 1):
+                go(0, p, b, 2 * near + c)
+                go(1, p, b, 2 * side + c)
+            for p in (2 * t, 2 * t + 1):
+                go(3, p, b, mate)
+        arrived(0, b)
+        for p in pieces:
+            sent[3, p].wait_recv()
+        arrived(1, mate)
+        for p in pieces:
+            sent[0, p].wait_recv()
+            go(2, p, 2 * near + c, 2 * side + c)
+            go(4, p, 2 * near + c, mate)
+        arrived(2, 2 * near + c)
+        for p in pieces:
+            sent[1, p].wait_recv()
+            go(5, p, 2 * side + c, mate)
+        arrived(3, 2 * side + c)
+        for p in pieces:
+            sent[2, p].wait_recv()
+            go(6, p, 2 * diagonal + c, mate)
+        for p in pieces:
+            sent[4, p].wait_recv()
+        arrived(4, 2 * side + 1 - c)
+        for p in pieces:
+            sent[5, p].wait_recv()
+        arrived(5, 2 * near + 1 - c)
+        arrived(6, 2 * diagonal + c)
+        for p in pieces:
+            sent[6, p].wait_recv()
+        arrived(7, 2 * diagonal + 1 - c)
+        return list(sent.values())
+
+    def gather(g, arrived, ready=lambda t: None):
+        if paired and n == 8:
+            return square(g, arrived, ready)
+        for t in range(2):
+            ready(t)
         if paired:
             q, c = b // 2, lax.rem(b, 2)
             mate = 2 * q + 1 - c
@@ -113,8 +178,8 @@
     def accumulate(g, where, first):
         d, m = buf[g, 0, where, :], buf[g, 1, where, :]
         for p in range(2):
-            top = mm(sl[0, p, :, where], m) - mm(dl[0, p, :, where], d)
-            low = mm(hy[0, p, :, where], d) + mm(ad[0, p, :, where], m)
+            top = mm(sl[p, :, where], m) - mm(dl[p, :, where], d)
+            low = mm(hy[p, :, where], d) + mm(ad[p, :, where], m)
             acc[p] = top if first else acc[p] + top
             acc[2 + p] = low if first else acc[2 + p] + low
 
@@ -139,9 +204,14 @@
 
         def first_arrival(count, owner):
             where = block_of(owner)
+            if count == 0:
+                @pl.when(k == 0)
+                def _():
+                    for one in loads:
+                        one.wait()
             if chunked:
                 pick(where, count == 0)
-                if count < n // 2:
+                if count < n - 2:
                     accumulate(0, where, count == 0)
                 else:
                     held.append(where)
@@ -178,7 +248,8 @@
 
         coupled = mm(spread_sel[...], xr[...])
         width = buf.shape[3]
-        for t in range(2):
+
+        def store_middle(t):
             sign = -0.5 if t == 0 else 0.5
             middle = acc[2 * t] + turned(acc[2 * t + 1]) + sign * coupled[:, t * width:(t + 1) * width]
             buf[1, t, own, :] = middle.astype(jnp.bfloat16)
@@ -187,7 +258,7 @@
             if chunked:
                 accumulate(1, block_of(owner), count == 0)
 
-        sends = gather(1, second_arrival)
+        sends = gather(1, second_arrival, store_middle)
         if not chunked:
             accumulate(1, everything, True)
         for t in range(2):
@@ -290,9 +361,9 @@
     out = pl.pallas_call(
         functools.partial(kernel, ns, n, paired),
         out_shape=jax.ShapeDtypeStruct((2, rows, width), jnp.float32),
-        in_specs=[vmem] * 8,
+        in_specs=[pl.BlockSpec(memory_space=pl.ANY)] * 4 + [vmem] * 4,
         out_specs=vmem,
-        scratch_shapes=[
+        scratch_shapes=[pltpu.VMEM((2, rows, total), jnp.bfloat16)] * 4 + [
             pltpu.VMEM((2, 2, total, width), jnp.bfloat16),
             pltpu.VMEM((4, rows, width), jnp.float32),
             pltpu.VMEM((rows, total), jnp.bfloat16),
@@ -305,8 +376,8 @@
             pltpu.VMEM((BASIS + 1, 8, width), jnp.float32),
             pltpu.VMEM((2, n, 8, width), jnp.float32),
             pltpu.VMEM((2, ns, 8, width), jnp.float32),
-            dma((2, n)), dma((2, n)), dma((2,)), dma((2,)),
-            dma((2, n)), dma((2, n)), dma((2, ns)), dma((2, ns)),
+            dma((2, 4 * n)), dma((2, 4 * n)), dma((2,)), dma((2,)),
+            dma((2, n)), dma((2, n)), dma((2, ns)), dma((2, ns)), dma((4,)),
         ],
         compiler_params=pltpu.CompilerParams(
             collective_id=0, has_side_effects=True, vmem_limit_bytes=48 * 1024 * 1024),

time: 197 us -> 184 us (0.934)
  Pallas kernels: 190 us -> 177 us
    pallas_call x1, Pallas kernels: 190 us -> 177 us  [body(): pl.pallas_call(functools.partial(kernel, ns, n, paired), out_shape=jax.Sh...]
where the time goes in v2:
time: 184 us; the launch traced here: 183 us
  Pallas kernels  177 us (96%)
  local copies, waits for them, and re-layouts  4.63 us (3%)
    pallas_call x1, Pallas kernels, body(): pl.pallas_call(functools.partial(kernel, ns, n, paired), out_shape=jax.Sh...  177 us

profile of v2, /device:TPU:0, one launch (start us, length us, event | category | flops | bytes accessed | tf_op | source)
XLA Modules:
  0.0 183.3 jit_solution(11880025331273438818)
XLA Ops:
  0.0 0.0 copy-start.2
  0.0 0.0 copy-start
  0.0 0.9 fusion.1
  0.9 0.7 fusion
  1.6 0.1 copy.13.up
  1.8 0.2 copy.17
  2.0 0.3 reshape.7.down
  2.3 0.0 copy-done.2
  2.4 0.2 copy.14.rhs
  2.6 1.1 copy.15.start
  3.7 0.0 copy-done
  3.7 0.0 copy-start.1
  3.7 1.6 copy-done.1
  5.3 176.9 %shard_map.73 = f32[2,256,128]{2,1,0:T(8,128)S(1)} custom-call(bf16[1,2,256,2048]{3,2,1,0:T(8,128)(2,1)S(1)} %copy-done, bf16[1,2,256,2048]{3,2,1,0:T(8,128)(2,1)S(1)} %copy-done.1, bf16[1,2,256,2048]{3,2,1,0:T(8,128)(2,1)} %hy_in.1, bf16[1,2,256,2048]{3,2,1,0:T(8,128)(2,1)} %ad_in.1, s32[128,1]{1,0:T(8,128)S(1)} %copy.13.up, s32[1,2048]{1,0:T(1,128)S(1)} %reshape.7.down, ...), custom_call_target="tpu_custom_call" | custom-call | tf_op jit(solution)/shard_map/pallas_call | solution.py:361
  182.2 0.1 slice_bitcast_fusion.1
  182.4 0.9 copy.16
  (2 shorter events, 0.1 us)
Async XLA Ops:
  0.0 2.3 %copy-start.2 = (f32[1,2,2,256,64]{3,4,2,1,0:T(8,128)S(1)}, f32[1,2,2,256,64]{3,4,2,1,0:T(8,128)}, u32[]{:S(2)}) copy-start(f32[1,2,2,256,64]{3,4,2,1,0:T(8,128)} %param.12) | copy-start | bytes 786436
  0.0 3.7 %copy-start = (bf16[1,2,256,2048]{3,2,1,0:T(8,128)(2,1)S(1)}, bf16[1,2,256,2048]{3,2,1,0:T(8,128)(2,1)}, u32[]{:S(2)}) copy-start(bf16[1,2,256,2048]{3,2,1,0:T(8,128)(2,1)} %dl_in.1) | copy-start | bytes 6291460
  3.7 1.6 copy-start.1

commit v3 on v2

--- a/solution.py
+++ b/solution.py
@@ -216,7 +216,18 @@
                 else:
                     held.append(where)
 
-        sends = gather(0, first_arrival)
+        def next_vector(t):
+            @pl.when(k > 0)
+            def _():
+                past = coef[k - 1]
+                w = img[t]
+                for i in range(BASIS):
+                    w = w - past[i:i + 1] * basis[i, t]
+                w = w * (1.0 / past[BASIS:BASIS + 1])
+                basis[k - 1, t] = w
+                buf[0, t, own, :] = w.astype(jnp.bfloat16)
+
+        sends = gather(0, first_arrival, next_vector)
         if not chunked:
             pick(everything, True)
         xs[...] = y[...].astype(jnp.bfloat16)
@@ -298,14 +309,6 @@
             squares = squares - summed[i:i + 1] * summed[i:i + 1]
         height = jnp.sqrt(jnp.maximum(squares, 0.0) + EPSILON)
         coef[k] = jnp.concatenate([summed[:BASIS], height, jnp.zeros((2, height.shape[1]), jnp.float32)], axis=0)
-        scale = 1.0 / height
-        for t in range(2):
-            w = img[t]
-            for i in range(BASIS):
-                w = w - summed[i:i + 1] * basis[i, t]
-            w = w * scale
-            basis[k, t] = w
-            buf[0, t, own, :] = w.astype(jnp.bfloat16)
         return carry
 
     lax.fori_loop(0, BASIS + 1, step, 0)
@@ -372,7 +375,7 @@
             pltpu.VMEM((rows, 2 * width), jnp.bfloat16),
             pltpu.VMEM((rows, 2 * width), jnp.float32),
             pltpu.VMEM((2, rows, width), jnp.float32),
-            pltpu.VMEM((BASIS + 1, 2, rows, width), jnp.float32),
+            pltpu.VMEM((BASIS, 2, rows, width), jnp.float32),
             pltpu.VMEM((BASIS + 1, 8, width), jnp.float32),
             pltpu.VMEM((2, n, 8, width), jnp.float32),
             pltpu.VMEM((2, ns, 8, width), jnp.float32),

time: 184 us -> 183 us (level)
  no operation moved by 1% of the time
where the time goes in v3:
time: 183 us
  Pallas kernels  176 us (96%)
  local copies, waits for them, and re-layouts  4.63 us (3%)
    pallas_call x1, Pallas kernels, body(): pl.pallas_call(functools.partial(kernel, ns, n, paired), out_shape=jax.Sh...  176 us

profile of v3, /device:TPU:0, one launch (start us, length us, event | category | flops | bytes accessed | tf_op | source)
XLA Modules:
  0.0 182.7 jit_solution(17897358314054301473)
XLA Ops:
  0.0 0.0 copy-start.2
  0.0 0.0 copy-start
  0.0 0.9 fusion.1
  0.9 0.7 fusion
  1.6 0.1 copy.13.up
  1.8 0.2 copy.17
  2.0 0.3 reshape.7.down
  2.3 0.0 copy-done.2
  2.4 0.2 copy.14.rhs
  2.6 1.1 copy.15.start
  3.7 0.0 copy-done
  3.7 0.0 copy-start.1
  3.7 1.6 copy-done.1
  5.3 176.3 %shard_map.73 = f32[2,256,128]{2,1,0:T(8,128)S(1)} custom-call(bf16[1,2,256,2048]{3,2,1,0:T(8,128)(2,1)S(1)} %copy-done, bf16[1,2,256,2048]{3,2,1,0:T(8,128)(2,1)S(1)} %copy-done.1, bf16[1,2,256,2048]{3,2,1,0:T(8,128)(2,1)} %hy_in.1, bf16[1,2,256,2048]{3,2,1,0:T(8,128)(2,1)} %ad_in.1, s32[128,1]{1,0:T(8,128)S(1)} %copy.13.up, s32[1,2048]{1,0:T(1,128)S(1)} %reshape.7.down, ...), custom_call_target="tpu_custom_call" | custom-call | tf_op jit(solution)/shard_map/pallas_call | solution.py:364
  181.7 0.1 slice_bitcast_fusion.1
  181.8 0.9 copy.16
  (2 shorter events, 0.1 us)
Async XLA Ops:
  0.0 2.3 %copy-start.2 = (f32[1,2,2,256,64]{3,4,2,1,0:T(8,128)S(1)}, f32[1,2,2,256,64]{3,4,2,1,0:T(8,128)}, u32[]{:S(2)}) copy-start(f32[1,2,2,256,64]{3,4,2,1,0:T(8,128)} %param.12) | copy-start | bytes 786436
  0.0 3.7 %copy-start = (bf16[1,2,256,2048]{3,2,1,0:T(8,128)(2,1)S(1)}, bf16[1,2,256,2048]{3,2,1,0:T(8,128)(2,1)}, u32[]{:S(2)}) copy-start(bf16[1,2,256,2048]{3,2,1,0:T(8,128)(2,1)} %dl_in.1) | copy-start | bytes 6291460
  3.7 1.6 copy-start.1
